TPU v7x, 256 devices: a whole 4x4x8 slice. The times are simulated.
256 devices in a mesh: frow: 8 (over y, x_lo), fcol: 32 (over z, x_hi, core).
Axes of the slice: x: 4 (x_hi: 2, x_lo: 2; x = x_hi * 2 + x_lo), y: 4, z: 8, core: 2. Of those that a mesh axis runs over, the one named last changes fastest.
Arguments:
- science: float32 [4, 1024, 4096], P(None, 'frow', 'fcol')
- pixel_mask: int32 [4, 1024, 4096], P(None, 'frow', 'fcol'), may hold values from 0 to 3, as said below
- coadd_image: float32 [1024, 4096], P('frow', 'fcol')
- coadd_variance: float32 [1024, 4096], P('frow', 'fcol'), may hold values from 0.5 to 2
- dither: int32 [4, 2], replicated, may hold values from -113 to 113, as said below
- stamps: int32 [4, 8, 32, 12], P(None, 'frow', 'fcol'), may hold values from -1 to 15, as said below
Outputs:
- scaled_difference: float32 [4, 1024, 4096], P(None, 'frow', 'fcol')
Inputs may be any that keep to these rules, and one draw needn't show every extreme that they name: `pixel_mask`: 0 marks a usable pixel; 1 a bad one, 2 a saturated one, 3 both. dither[v, 0] is the row offset and dither[v, 1] the column offset of visit v. `stamps`: cell numbers, row-major over the (4) x (4) cells of the tile; distinct within a tile and visit; live entries first, then -1; at least 4 live entries, and every visit has a tile with all 12 live.
All inputs are finite; a program needn't handle non-finite values.
Results may differ from a plain program's by a relative error of at most 0.023.
Values sent between devices are 32-bit elements; how exact they have to be, the bound alone decides.
No kernel may reach another device: no remote copies, remote signals or barrier semaphores. Data moves between devices by JAX's collectives and lax.ppermute only.
A program may use at most 128 MiB of HBM per device.

v0:
```python
import jax
import jax.numpy as jnp
from jax import lax
from jax.sharding import PartitionSpec as P

V = 4
TH = 128
TW = 128
R = 15
NB = 30
STAMP = 32
DMAX = 113
SPREADS = (0.75, 1.5, 3.0)


def with_halo(block, sides, width):
    for axis, dim in sides:
        count = lax.axis_size(axis)
        forward = [(i, i + 1) for i in range(count - 1)]
        backward = [(target, source) for source, target in forward]
        low = lax.ppermute(
            lax.slice_in_dim(block, block.shape[dim] - width, None, axis=dim), axis, forward
        )
        high = lax.ppermute(lax.slice_in_dim(block, 0, width, axis=dim), axis, backward)
        block = jnp.concatenate([low, block, high], axis=dim)
    return block


def kernel_table(radius):
    offsets = jnp.arange(-radius, radius + 1, dtype=jnp.float32)
    profiles = []
    for spread in SPREADS:
        for degree in range(4):
            profile = (
                jnp.exp(-offsets * offsets / (2.0 * spread * spread)) * (offsets / spread) ** degree
            )
            profiles.append(profile / jnp.sqrt(jnp.sum(profile * profile)))
    return jnp.stack(profiles).astype(jnp.bfloat16)


def basis_pairs():
    along_rows = []
    along_cols = []
    for family in range(3):
        for row_degree in range(4):
            for col_degree in range(4 - row_degree):
                along_rows.append(family * 4 + row_degree)
                along_cols.append(family * 4 + col_degree)
    return (along_rows, along_cols)


def solve_fit(normal_matrix, normal_vector):
    unknowns = normal_matrix.shape[-1]
    trace_sum = jnp.einsum("fii->f", normal_matrix)
    ridge_term = 0.001 * trace_sum / unknowns
    shifted = normal_matrix + ridge_term[:, None, None] * jnp.eye(unknowns, dtype=jnp.float32)
    factor = jnp.linalg.cholesky(shifted)
    solved = jax.scipy.linalg.cho_solve((factor, True), normal_vector[..., None])[..., 0]
    return solved.reshape(normal_matrix.shape[0], 3, unknowns // 3)


def toeplitz_table(rows_out, table):
    tap_count = 2 * R + 1
    offsets = jnp.arange(rows_out + 2 * R)[None, :] - jnp.arange(rows_out)[:, None]
    inside = (offsets >= 0) & (offsets < tap_count)
    clipped = jnp.clip(offsets, 0, tap_count - 1)
    return jnp.where(inside[None], table[:, clipped], jnp.zeros((), jnp.bfloat16))


def on_device(science, pixel_mask, coadd_image, coadd_variance, dither, stamps):
    highest = lax.Precision.HIGHEST
    margin = DMAX + R
    planes = jnp.stack([coadd_image, coadd_variance])
    padded = with_halo(planes, (("frow", 1), ("fcol", 2)), margin)
    padded_image = padded[0].astype(jnp.bfloat16)
    padded_var = padded[1]
    table = kernel_table(R)
    along_rows, along_cols = basis_pairs()
    block_cols = min(128, TW)
    block_rows = min(128, TH)
    col_offsets = jnp.arange(block_cols + 2 * R)[:, None] - jnp.arange(block_cols)[None, :]
    col_inside = (col_offsets >= 0) & (col_offsets <= 2 * R)
    col_toeplitz = jnp.where(
        col_inside[None], table[:, jnp.clip(col_offsets, 0, 2 * R)], jnp.zeros((), jnp.bfloat16)
    )
    row_toeplitz = toeplitz_table(block_rows, table[jnp.array(along_rows)])
    column_choice = jnp.array(along_cols)
    cells_down = TH // STAMP
    cells_across = TW // STAMP
    cell_total = cells_down * cells_across
    half_rows = TH / 2.0
    half_cols = TW / 2.0
    row_coord = (jnp.arange(TH, dtype=jnp.float32) + 0.5 - half_rows) / half_rows
    col_coord = (jnp.arange(TW, dtype=jnp.float32) + 0.5 - half_cols) / half_cols
    row_flat = jnp.broadcast_to(row_coord[:, None], (TH, TW)).reshape(TH * TW)
    col_flat = jnp.broadcast_to(col_coord[None, :], (TH, TW)).reshape(TH * TW)
    cell_number = jnp.arange(cell_total, dtype=jnp.int32)
    cell_row = cell_number // cells_across
    cell_col = cell_number % cells_across
    centre_row = (cell_row * STAMP + STAMP / 2.0 - half_rows) / half_rows
    centre_col = (cell_col * STAMP + STAMP / 2.0 - half_cols) / half_cols
    spatial = jnp.stack([jnp.ones_like(centre_row), centre_col, centre_row]).astype(jnp.float32)

    def cell_planes(plane):
        return (
            plane.reshape(cells_down, STAMP, cells_across, STAMP)
            .transpose(0, 2, 1, 3)
            .reshape(cell_total, STAMP * STAMP)
        )

    basis_list = []
    var_windows = []
    usable_list = []
    normal_matrices = []
    normal_vectors = []
    for v in range(V):
        row_shift = dither[v, 0]
        col_shift = dither[v, 1]
        window = lax.dynamic_slice(
            padded_image, (DMAX + row_shift, DMAX + col_shift), (TH + 2 * R, TW + 2 * R)
        )
        pieces = jnp.stack([window], axis=1)
        column_pass = jnp.einsum(
            "hbj,fjx->fhbx", pieces, col_toeplitz, preferred_element_type=jnp.float32
        )
        column_pass = column_pass.astype(jnp.bfloat16).reshape(12, TH + 2 * R, TW)
        chosen = column_pass[column_choice]
        blocks = jnp.einsum(
            "kyj,kjx->kyx", row_toeplitz, chosen, preferred_element_type=jnp.float32
        ).astype(jnp.bfloat16)
        var_window = lax.dynamic_slice(
            padded_var, (margin + row_shift, margin + col_shift), (TH, TW)
        )
        usable = (pixel_mask[v] == 0).astype(jnp.float32)
        weight = usable / (0.25 + var_window)
        basis_cells = (
            blocks.reshape(NB, cells_down, STAMP, cells_across, STAMP)
            .transpose(1, 3, 0, 2, 4)
            .reshape(cell_total, NB, STAMP * STAMP)
        )
        ones_row = jnp.ones((cell_total, 1, STAMP * STAMP), jnp.bfloat16)
        design = jnp.concatenate([basis_cells, ones_row], axis=1)
        weighted = (design * cell_planes(weight)[:, None, :]).astype(jnp.bfloat16)
        gram_cells = jnp.einsum(
            "ckp,clp->ckl", weighted, design, preferred_element_type=jnp.float32
        )
        right_cells = jnp.einsum(
            "ckp,cp->ck",
            weighted,
            cell_planes(science[v]).astype(jnp.bfloat16),
            preferred_element_type=jnp.float32,
        )
        cell_list = stamps[v, 0, 0]
        cell_use = jnp.sum((cell_list[:, None] == cell_number[None, :]).astype(jnp.float32), axis=0)
        normal_matrix = jnp.einsum(
            "ac,bc,c,ckl->akbl", spatial, spatial, cell_use, gram_cells, precision=highest
        )
        normal_matrices.append(normal_matrix.reshape(3 * (NB + 1), 3 * (NB + 1)))
        normal_vectors.append(
            jnp.einsum("ac,c,ck->ak", spatial, cell_use, right_cells, precision=highest).reshape(
                3 * (NB + 1)
            )
        )
        basis_list.append(blocks)
        var_windows.append(var_window)
        usable_list.append(usable)
    all_coefficients = solve_fit(jnp.stack(normal_matrices), jnp.stack(normal_vectors))
    totals = []
    differences = []
    for v in range(V):
        coefficients = all_coefficients[v]
        coef_main = coefficients[:, :NB]
        coef_high = coef_main.astype(jnp.bfloat16)
        coef_low = (coef_main - coef_high.astype(jnp.float32)).astype(jnp.bfloat16)
        stacked = jnp.concatenate([coef_high, coef_low], axis=0)
        weighted_sums = jnp.dot(
            stacked, basis_list[v].reshape(NB, TH * TW), preferred_element_type=jnp.float32
        )
        combined = weighted_sums[:3] + weighted_sums[3:] + coefficients[:, NB : NB + 1]
        fitted_model = (combined[0] + col_flat * combined[1] + row_flat * combined[2]).reshape(
            TH, TW
        )
        difference = science[v] - fitted_model
        totals.append(jnp.sum(usable_list[v] * difference * difference))
        differences.append(difference)
    strip_totals = lax.psum(jnp.stack(totals), "fcol")
    pixel_count = TH * TW * lax.axis_size("fcol")
    scaled = [
        differences[v] * lax.rsqrt(strip_totals[v] / pixel_count + var_windows[v] + 1e-06)
        for v in range(V)
    ]
    return jnp.stack(scaled)


def solution(mesh):
    in_specs = (
        P(None, "frow", "fcol"),
        P(None, "frow", "fcol"),
        P("frow", "fcol"),
        P("frow", "fcol"),
        P(),
        P(None, "frow", "fcol", None),
    )
    out_specs = P(None, "frow", "fcol")
    return jax.shard_map(
        on_device, mesh=mesh, in_specs=in_specs, out_specs=out_specs, check_vma=False
    )
```

profile of v0, /device:TPU:24, one launch (start us, length us, event | category | flops | bytes accessed | tf_op | source)
XLA Modules:
  0.0 451.9 jit_solution(16221667498306995601)
XLA Ops:
  0.0 0.9 pad_maximum_fusion.3
  0.9 3.6 collective-permute-start.1
  4.5 2.3 collective-permute-start
  26.6 1.6 fusion.208
  28.5 1.0 fusion.207
  29.6 1.3 pad_clamp_fusion.2
  31.6 0.9 pad_maximum_fusion.1
  32.5 1.3 collective-permute-start.3
  33.8 3.1 collective-permute-start.2
  62.6 41.3 %gather_fusion.1 = bf16[20224,30]{1,0:T(8,128)(2,1)} fusion(bf16[30,31]{0,1:T(8,128)(2,1)S(1)} %copy.35, s32[20480]{0:T(1024)S(1)} %pad_clamp_fusion.1), kind=kCustom, calls=%fused_computation.1 | custom fusion | bytes 2507776 | tf_op jit(solution)/shard_map/gather | solution.py:67
  103.9 5.0 %copy.36 = bf16[20224,30]{0,1:T(8,128)(2,1)S(1)} copy(bf16[20224,30]{1,0:T(8,128)(2,1)} %gather_fusion.1) | data formatting | bytes 2426880 | tf_op jit(solution)/shard_map/gather | solution.py:67
  108.9 6.9 %reshape.890 = bf16[128,158,30]{1,0,2:T(8,128)(2,1)} reshape(bf16[20224,30]{0,1:T(8,128)(2,1)S(1)} %copy.36) | data formatting | bytes 2426880 | tf_op jit(solution)/shard_map/gather | solution.py:67
  115.8 41.0 %gather_fusion.2 = bf16[20224,12]{1,0:T(8,128)(2,1)} fusion(bf16[12,31]{0,1:T(8,128)(2,1)S(1)} %copy.37, s32[20480]{0:T(1024)S(1)} %pad_clamp_fusion), kind=kCustom, calls=%fused_computation.2 | custom fusion | bytes 1051648 | tf_op jit(solution)/shard_map/gather | solution.py:84
  156.8 4.2 copy.38
  163.7 1.0 gather_fusion.3
  164.8 1.9 gather_fusion.4
  166.6 2.4 fusion.8
  169.8 3.2 reshape.862
  173.2 3.2 reshape.865
  176.4 1.4 fusion.30
  177.8 1.9 gather_fusion.5
  179.6 2.5 fusion.14
  182.2 0.9 copy-done.1
  183.3 6.7 %reshape.868 = bf16[30,4,32,4,32]{4,3,2,1,0:T(4,128)(2,1)} reshape(bf16[30,128,128]{2,1,0:T(8,128)(2,1)} %copy-done.1) | data formatting | bytes 1966080 | tf_op jit(solution)/shard_map/reshape | solution.py:137
  190.0 2.2 fusion.31
  192.2 2.9 gather_fusion.6
  195.1 2.5 fusion.17
  197.6 1.0 copy-done
  198.6 1.1 pad.49
  199.7 6.3 %reshape.871 = bf16[30,4,32,4,32]{4,3,2,1,0:T(4,128)(2,1)} reshape(bf16[30,128,128]{2,1,0:T(8,128)(2,1)} %copy-done) | data formatting | bytes 1966080 | tf_op jit(solution)/shard_map/reshape | solution.py:137
  206.0 1.9 add_divide_fusion.3
  207.9 1.0 div.411
  209.6 1.7 mul.508
  211.3 1.0 div.417
  213.1 1.7 mul.517
  215.7 1.7 mul.514
  218.3 1.1 mul.511
  219.4 5.2 %copy.119 = bf16[30,4,32,4,32]{4,2,3,1,0:T(8,128)(2,1)} copy(bf16[30,4,32,4,32]{4,3,2,1,0:T(4,128)(2,1)} %reshape.862) | data formatting | bytes 1966080 | tf_op jit(solution)/shard_map/reshape | solution.py:137
  224.6 6.6 %reshape.863 = bf16[16,30,1024]{2,0,1:T(8,128)(2,1)} reshape(bf16[4,4,30,32,32]{4,3,1,0,2:T(8,128)(2,1)} %bitcast.342) | data formatting | bytes 1966080 | tf_op jit(solution)/shard_map/reshape | solution.py:139
  231.2 1.8 copy.41
  235.4 5.3 %copy.118 = bf16[30,4,32,4,32]{4,2,3,1,0:T(8,128)(2,1)} copy(bf16[30,4,32,4,32]{4,3,2,1,0:T(4,128)(2,1)} %reshape.865) | data formatting | bytes 1966080 | tf_op jit(solution)/shard_map/reshape | solution.py:137
  240.7 6.8 %reshape.866 = bf16[16,30,1024]{2,0,1:T(8,128)(2,1)} reshape(bf16[4,4,30,32,32]{4,3,1,0,2:T(8,128)(2,1)} %bitcast.343) | data formatting | bytes 1966080 | tf_op jit(solution)/shard_map/reshape | solution.py:139
  247.5 1.8 copy.46
  249.7 1.0 fusion.22
  251.9 0.9 fusion.100
  253.5 5.3 %copy.117 = bf16[30,4,32,4,32]{4,2,3,1,0:T(8,128)(2,1)} copy(bf16[30,4,32,4,32]{4,3,2,1,0:T(4,128)(2,1)} %reshape.868) | data formatting | bytes 1966080 | tf_op jit(solution)/shard_map/reshape | solution.py:137
  258.8 6.6 %reshape.869 = bf16[16,30,1024]{2,0,1:T(8,128)(2,1)} reshape(bf16[4,4,30,32,32]{4,3,1,0,2:T(8,128)(2,1)} %bitcast.344) | data formatting | bytes 1966080 | tf_op jit(solution)/shard_map/reshape | solution.py:139
  265.4 1.8 copy.51
  267.6 1.0 fusion.24
  269.8 0.9 fusion.98
  271.3 5.2 %copy.116 = bf16[30,4,32,4,32]{4,2,3,1,0:T(8,128)(2,1)} copy(bf16[30,4,32,4,32]{4,3,2,1,0:T(4,128)(2,1)} %reshape.871) | data formatting | bytes 1966080 | tf_op jit(solution)/shard_map/reshape | solution.py:137
  276.5 6.6 %reshape.872 = bf16[16,30,1024]{2,0,1:T(8,128)(2,1)} reshape(bf16[4,4,30,32,32]{4,3,1,0,2:T(8,128)(2,1)} %bitcast.345) | data formatting | bytes 1966080 | tf_op jit(solution)/shard_map/reshape | solution.py:139
  283.1 1.8 copy.56
  285.4 1.0 fusion.26
  291.4 0.9 fusion.96
  293.0 0.9 multiply_add_fusion
  294.7 1.1 fusion.75
  295.8 34.3 %custom-call.11 = f32[4,93,93]{2,1,0:T(8,128)S(1)} custom-call(f32[4,93,93]{2,1,0:T(8,128)S(1)} %fusion.75), custom_call_target="Cholesky" | custom-call | tf_op jit(solution)/shard_map/jit(cholesky)/cholesky | solution.py:57
  331.7 28.6 %custom-call.12 = f32[4,1,93,93]{2,3,1,0:T(8,128)S(1)} custom-call(f32[4,1,93,93]{3,2,1,0:T(8,128)S(1)} %select_bitcast_fusion), custom_call_target="InvertDiagBlocksLowerTriangular" | custom-call | tf_op jit(solution)/shard_map/jit(_cho_solve)/vmap()/triangular_solve | solution.py:58
  362.9 1.9 copy.87
  370.6 2.6 pad_maximum_fusion.6
  373.2 72.3 %psum.7 = f32[4]{0:T(128)S(1)} all-reduce(f32[4]{0:T(128)S(1)} %pad_maximum_fusion.6), channel_id=1, replica_groups=mesh['frow'=8,'fcol'=32] {'fcol'}, use_global_device_ids=true, to_apply=%region_23.24 | all-reduce | flops 4 | bytes 32 | tf_op jit(solution)/shard_map/psum | solution.py:186
  448.7 1.1 rsqrt_multiply_fusion.3
  449.8 1.1 rsqrt_multiply_fusion.1
  (213 shorter events, 49.8 us)
Async XLA Ops:
  0.9 30.7 %collective-permute-start.1 = (f32[2,128,128]{2,1,0:T(8,128)S(1)}, f32[2,128,128]{2,1,0:T(8,128)S(1)}, u32[]{:S(2)}, u32[]{:S(2)}) collective-permute-start(f32[2,128,128]{2,1,0:T(8,128)S(1)} %pad_maximum_fusion.3), channel_id=1, source_target_pairs={{32,0},{64,32},{96,64},{128,96},{160,128},{192,160},{224,192},{33,... | collective-permute-start | bytes 393224 | tf_op jit(solution)/shard_map/ppermute | solution.py:24
  4.5 27.2 %collective-permute-start = (f32[2,128,128]{2,1,0:T(8,128)S(1)}, f32[2,128,128]{2,1,0:T(8,128)S(1)}, u32[]{:S(2)}, u32[]{:S(2)}) collective-permute-start(f32[2,128,128]{2,1,0:T(8,128)S(1)} %pad_maximum_fusion.3), channel_id=1, source_target_pairs={{0,32},{32,64},{64,96},{96,128},{128,160},{160,192},{192,224},{1,3... | collective-permute-start | bytes 393224 | tf_op jit(solution)/shard_map/ppermute | solution.py:21
  14.7 146.6 %copy-start.29 = (f32[1,16]{1,0:T(1,128)}, f32[1,16]{1,0:T(1,128)S(1)}, u32[]{:S(2)}) copy-start(f32[1,16]{1,0:T(1,128)S(1)} %get-tuple-element.86) | copy-start | bytes 196
  14.7 146.6 %copy-start.31 = (f32[1,16]{1,0:T(1,128)}, f32[1,16]{1,0:T(1,128)S(1)}, u32[]{:S(2)}) copy-start(f32[1,16]{1,0:T(1,128)S(1)} %get-tuple-element.87) | copy-start | bytes 196
  16.5 146.8 %copy-start.23 = (pred[158,128]{1,0:T(8,128)(4,1)}, pred[158,128]{1,0:T(8,128)(4,1)S(1)}, u32[]{:S(2)}) copy-start(pred[158,128]{1,0:T(8,128)(4,1)S(1)} %fusion.90) | copy-start | bytes 60676
  29.6 131.7 %copy-start.33 = (f32[3]{0:T(128)}, f32[3]{0:T(128)S(1)}, u32[]{:S(2)}) copy-start(f32[3]{0:T(128)S(1)} %pad.36.clone) | copy-start | bytes 40
  31.6 129.6 %copy-start.35 = (f32[16]{0:T(128)}, f32[16]{0:T(128)S(1)}, u32[]{:S(2)}) copy-start(f32[16]{0:T(128)S(1)} %get-tuple-element.92) | copy-start | bytes 196
  31.6 129.6 %copy-start.36 = (f32[16]{0:T(128)}, f32[16]{0:T(128)S(1)}, u32[]{:S(2)}) copy-start(f32[16]{0:T(128)S(1)} %get-tuple-element.93) | copy-start | bytes 196
  32.5 129.4 %collective-permute-start.3 = (f32[2,384,128]{2,1,0:T(8,128)S(1)}, f32[2,384,128]{2,1,0:T(8,128)S(1)}, u32[]{:S(2)}, u32[]{:S(2)}) collective-permute-start(f32[2,384,128]{2,1,0:T(8,128)S(1)} %pad_maximum_fusion.1), channel_id=1, source_target_pairs={{1,0},{2,1},{3,2},{4,3},{5,4},{6,5},{7,6},{8,7},{9,8},{10,9},{11,1... | collective-permute-start | bytes 1179656 | tf_op jit(solution)/shard_map/ppermute | solution.py:24
  33.8 128.1 %collective-permute-start.2 = (f32[2,384,128]{2,1,0:T(8,128)S(1)}, f32[2,384,128]{2,1,0:T(8,128)S(1)}, u32[]{:S(2)}, u32[]{:S(2)}) collective-permute-start(f32[2,384,128]{2,1,0:T(8,128)S(1)} %pad_maximum_fusion.1), channel_id=1, source_target_pairs={{0,1},{1,2},{2,3},{3,4},{4,5},{5,6},{6,7},{7,8},{8,9},{9,10},{10,1... | collective-permute-start | bytes 1179656 | tf_op jit(solution)/shard_map/ppermute | solution.py:21
  156.8 5.2 %copy-start.5 = (f32[128,128]{1,0:T(8,128)S(1)}, f32[128,128]{1,0:T(8,128)}, u32[]{:S(2)}) copy-start(f32[128,128]{1,0:T(8,128)} %param.11) | copy-start | bytes 196612
  156.8 5.2 %copy-start.6 = (f32[128,128]{1,0:T(8,128)S(1)}, f32[128,128]{1,0:T(8,128)}, u32[]{:S(2)}) copy-start(f32[128,128]{1,0:T(8,128)} %param.10) | copy-start | bytes 196612
  161.0 2.4 copy-start.7
  161.2 0.9 copy-start.38
  161.2 0.9 copy-start.39
  163.7 2.9 copy-start.21
  166.6 2.4 copy-start.2
  166.6 2.5 copy-start.4
  173.2 3.2 copy-start.24
  176.4 3.3 copy-start.22
  182.2 1.0 copy-start.1
  197.6 1.0 copy-start
  199.7 6.3 %copy-start.8 = (s32[4,128,128]{2,1,0:T(8,128)S(1)}, s32[4,128,128]{2,1,0:T(8,128)}, u32[]{:S(2)}) copy-start(s32[4,128,128]{2,1,0:T(8,128)} %param.9) | copy-start | bytes 786436
  231.2 1.8 copy-start.15
  231.2 2.3 copy-start.12
  233.0 0.9 copy-start.19
  233.0 0.9 copy-start.28
  233.0 1.5 copy-start.30
  233.0 1.5 copy-start.32
  233.0 1.5 copy-start.34
  233.1 1.5 copy-start.37
  247.5 2.2 copy-start.11
  249.2 1.4 copy-start.27
  265.4 1.8 copy-start.14
  265.4 2.2 copy-start.10
  267.2 1.4 copy-start.26
  283.1 1.8 copy-start.13
  283.1 2.2 copy-start.9
  284.9 1.4 copy-start.25
  368.1 1.0 copy-start.3
  368.2 1.0 copy-start.18
  368.2 0.9 copy-start.20
  368.2 1.6 copy-start.16
  368.2 1.6 copy-start.17
where the time goes:
time: 457 us; the launch traced here: 452 us
  local copies, waits for them, and re-layouts  219 us (48%)
  other arithmetic  94.4 us (21%)
  blocking collectives  72.3 us (16%)
  between operations  32.4 us (7%)
  matrix products  24 us (5%)
  starting transfers between devices  10.2 us (2%)
    psum x1, blocking collectives, on_device(): strip_totals = lax.psum(jnp.stack(totals), 'fcol')  72.3 us
    gather x3, local copies, waits for them, and re-layouts, toeplitz_table(): table[:, clipped]  53.2 us
    gather x2, local copies, waits for them, and re-layouts, on_device(): table[:, jnp.clip(col_offsets, 0, 2 * R)]  45.2 us
    reshape x8, local copies, waits for them, and re-layouts, on_device(): blocks.reshape(NB, cells_down, STAMP, cells_across, STAMP)  40.4 us
    another operation x4, other arithmetic, solve_fit(): factor = jnp.linalg.cholesky(shifted)  35.8 us
    reshape x8, local copies, waits for them, and re-layouts, on_device(): basis_cells = blocks.reshape(NB, cells_down, STAMP, cells_across, STAMP)....  33.7 us
    another operation x3, other arithmetic, solve_fit(): jax.scipy.linalg.cho_solve((factor, True), normal_vector[..., None])[..., 0]  30 us
    unnamed x91, local copies, waits for them, and re-layouts  9.34 us
  transfers between devices with their start and end apart: 4, of which 0 were waited for; matrix products, arithmetic and copies ran while one was open for 27% of the time, Pallas kernels for 0%

commit v1 on v0

--- a/solution.py
+++ b/solution.py
@@ -183,7 +183,7 @@
         difference = science[v] - fitted_model
         totals.append(jnp.sum(usable_list[v] * difference * difference))
         differences.append(difference)
-    strip_totals = lax.psum(jnp.stack(totals), "fcol")
+    strip_totals = jnp.sum(lax.all_gather(jnp.stack(totals), "fcol"), axis=0)
     pixel_count = TH * TW * lax.axis_size("fcol")
     scaled = [
         differences[v] * lax.rsqrt(strip_totals[v] / pixel_count + var_windows[v] + 1e-06)

time: 457 us -> 458 us (level)
    psum x1 -> x0, blocking collectives: 72.3 us -> none  [on_device(): strip_totals = lax.psum(jnp.stack(totals), 'fcol')]
    unnamed x0 -> x1, blocking collectives: none -> 72.3 us
    unnamed x91 -> x95, local copies, waits for them, and re-layouts: 9.34 us -> 10 us
where the time goes in v1:
time: 458 us; the launch traced here: 453 us
  local copies, waits for them, and re-layouts  219 us (48%)
  other arithmetic  94.5 us (21%)
  blocking collectives  72.3 us (16%)
  between operations  32.6 us (7%)
  matrix products  24 us (5%)
  starting transfers between devices  10.2 us (2%)
    unnamed x1, blocking collectives  72.3 us
    gather x3, local copies, waits for them, and re-layouts, toeplitz_table(): table[:, clipped]  53.2 us
    gather x2, local copies, waits for them, and re-layouts, on_device(): table[:, jnp.clip(col_offsets, 0, 2 * R)]  45.2 us
    reshape x8, local copies, waits for them, and re-layouts, on_device(): blocks.reshape(NB, cells_down, STAMP, cells_across, STAMP)  40.4 us
    another operation x4, other arithmetic, solve_fit(): factor = jnp.linalg.cholesky(shifted)  35.8 us
    reshape x8, local copies, waits for them, and re-layouts, on_device(): basis_cells = blocks.reshape(NB, cells_down, STAMP, cells_across, STAMP)....  33.7 us
    another operation x3, other arithmetic, solve_fit(): jax.scipy.linalg.cho_solve((factor, True), normal_vector[..., None])[..., 0]  30 us
    unnamed x95, local copies, waits for them, and re-layouts  10 us
  transfers between devices with their start and end apart: 4, of which 0 were waited for; matrix products, arithmetic and copies ran while one was open for 27% of the time, Pallas kernels for 0%

profile of v1, /device:TPU:24, one launch (start us, length us, event | category | flops | bytes accessed | tf_op | source)
XLA Modules:
  0.0 452.9 jit_solution(3965137220528597144)
XLA Ops:
  0.0 0.9 pad_maximum_fusion.3
  0.9 3.6 collective-permute-start.1
  4.5 2.3 collective-permute-start
  26.6 1.6 fusion.208
  28.5 1.0 fusion.207
  29.6 1.3 pad_clamp_fusion.2
  31.6 0.9 pad_maximum_fusion.1
  32.5 1.3 collective-permute-start.3
  33.8 3.1 collective-permute-start.2
  62.0 41.3 %gather_fusion.1 = bf16[20224,30]{1,0:T(8,128)(2,1)} fusion(bf16[30,31]{0,1:T(8,128)(2,1)S(1)} %copy.35, s32[20480]{0:T(1024)S(1)} %pad_clamp_fusion.1), kind=kCustom, calls=%fused_computation.1 | custom fusion | bytes 2507776 | tf_op jit(solution)/shard_map/gather | solution.py:67
  103.3 5.0 %copy.36 = bf16[20224,30]{0,1:T(8,128)(2,1)S(1)} copy(bf16[20224,30]{1,0:T(8,128)(2,1)} %gather_fusion.1) | data formatting | bytes 2426880 | tf_op jit(solution)/shard_map/gather | solution.py:67
  108.4 6.9 %reshape.890 = bf16[128,158,30]{1,0,2:T(8,128)(2,1)} reshape(bf16[20224,30]{0,1:T(8,128)(2,1)S(1)} %copy.36) | data formatting | bytes 2426880 | tf_op jit(solution)/shard_map/gather | solution.py:67
  115.2 41.0 %gather_fusion.2 = bf16[20224,12]{1,0:T(8,128)(2,1)} fusion(bf16[12,31]{0,1:T(8,128)(2,1)S(1)} %copy.37, s32[20480]{0:T(1024)S(1)} %pad_clamp_fusion), kind=kCustom, calls=%fused_computation.2 | custom fusion | bytes 1051648 | tf_op jit(solution)/shard_map/gather | solution.py:84
  156.3 4.2 copy.38
  164.5 1.0 gather_fusion.3
  165.6 1.9 gather_fusion.4
  167.4 2.4 fusion.8
  170.6 3.2 reshape.862
  174.0 3.2 reshape.865
  177.2 1.4 fusion.30
  178.6 1.9 gather_fusion.5
  180.5 2.5 fusion.14
  183.0 0.9 copy-done.1
  184.1 6.7 %reshape.868 = bf16[30,4,32,4,32]{4,3,2,1,0:T(4,128)(2,1)} reshape(bf16[30,128,128]{2,1,0:T(8,128)(2,1)} %copy-done.1) | data formatting | bytes 1966080 | tf_op jit(solution)/shard_map/reshape | solution.py:137
  190.8 2.2 fusion.31
  193.0 2.9 gather_fusion.6
  195.9 2.5 fusion.17
  198.4 1.0 copy-done
  199.4 1.1 pad.49
  200.5 6.3 %reshape.871 = bf16[30,4,32,4,32]{4,3,2,1,0:T(4,128)(2,1)} reshape(bf16[30,128,128]{2,1,0:T(8,128)(2,1)} %copy-done) | data formatting | bytes 1966080 | tf_op jit(solution)/shard_map/reshape | solution.py:137
  206.8 1.9 add_divide_fusion.3
  208.7 1.0 div.411
  210.4 1.7 mul.508
  212.1 1.0 div.417
  213.9 1.7 mul.517
  216.5 1.7 mul.514
  219.1 1.1 mul.511
  220.2 5.2 %copy.119 = bf16[30,4,32,4,32]{4,2,3,1,0:T(8,128)(2,1)} copy(bf16[30,4,32,4,32]{4,3,2,1,0:T(4,128)(2,1)} %reshape.862) | data formatting | bytes 1966080 | tf_op jit(solution)/shard_map/reshape | solution.py:137
  225.4 6.6 %reshape.863 = bf16[16,30,1024]{2,0,1:T(8,128)(2,1)} reshape(bf16[4,4,30,32,32]{4,3,1,0,2:T(8,128)(2,1)} %bitcast.343) | data formatting | bytes 1966080 | tf_op jit(solution)/shard_map/reshape | solution.py:139
  232.0 1.8 copy.41
  236.2 5.3 %copy.118 = bf16[30,4,32,4,32]{4,2,3,1,0:T(8,128)(2,1)} copy(bf16[30,4,32,4,32]{4,3,2,1,0:T(4,128)(2,1)} %reshape.865) | data formatting | bytes 1966080 | tf_op jit(solution)/shard_map/reshape | solution.py:137
  241.5 6.8 %reshape.866 = bf16[16,30,1024]{2,0,1:T(8,128)(2,1)} reshape(bf16[4,4,30,32,32]{4,3,1,0,2:T(8,128)(2,1)} %bitcast.344) | data formatting | bytes 1966080 | tf_op jit(solution)/shard_map/reshape | solution.py:139
  248.3 1.8 copy.46
  250.5 1.0 fusion.22
  252.7 0.9 fusion.100
  254.3 5.3 %copy.117 = bf16[30,4,32,4,32]{4,2,3,1,0:T(8,128)(2,1)} copy(bf16[30,4,32,4,32]{4,3,2,1,0:T(4,128)(2,1)} %reshape.868) | data formatting | bytes 1966080 | tf_op jit(solution)/shard_map/reshape | solution.py:137
  259.6 6.6 %reshape.869 = bf16[16,30,1024]{2,0,1:T(8,128)(2,1)} reshape(bf16[4,4,30,32,32]{4,3,1,0,2:T(8,128)(2,1)} %bitcast.345) | data formatting | bytes 1966080 | tf_op jit(solution)/shard_map/reshape | solution.py:139
  266.2 1.8 copy.51
  268.4 1.0 fusion.24
  270.6 0.9 fusion.98
  272.1 5.2 %copy.116 = bf16[30,4,32,4,32]{4,2,3,1,0:T(8,128)(2,1)} copy(bf16[30,4,32,4,32]{4,3,2,1,0:T(4,128)(2,1)} %reshape.871) | data formatting | bytes 1966080 | tf_op jit(solution)/shard_map/reshape | solution.py:137
  277.3 6.6 %reshape.872 = bf16[16,30,1024]{2,0,1:T(8,128)(2,1)} reshape(bf16[4,4,30,32,32]{4,3,1,0,2:T(8,128)(2,1)} %bitcast.346) | data formatting | bytes 1966080 | tf_op jit(solution)/shard_map/reshape | solution.py:139
  283.9 1.8 copy.56
  286.2 1.0 fusion.26
  292.2 0.9 fusion.96
  293.8 0.9 multiply_add_fusion
  295.5 1.1 fusion.75
  296.6 34.3 %custom-call.11 = f32[4,93,93]{2,1,0:T(8,128)S(1)} custom-call(f32[4,93,93]{2,1,0:T(8,128)S(1)} %fusion.75), custom_call_target="Cholesky" | custom-call | tf_op jit(solution)/shard_map/jit(cholesky)/cholesky | solution.py:57
  332.5 28.6 %custom-call.12 = f32[4,1,93,93]{2,3,1,0:T(8,128)S(1)} custom-call(f32[4,1,93,93]{3,2,1,0:T(8,128)S(1)} %select_bitcast_fusion), custom_call_target="InvertDiagBlocksLowerTriangular" | custom-call | tf_op jit(solution)/shard_map/jit(_cho_solve)/vmap()/triangular_solve | solution.py:58
  363.7 1.9 copy.87
  371.4 2.7 maximum_dynamic-update-slice_fusion
  374.1 72.3 %all-reduce.4 = f32[128]{0:T(128)S(1)} all-reduce(f32[128]{0:T(128)S(1)} %maximum_dynamic-update-slice_fusion), channel_id=2, replica_groups=mesh['frow'=8,'fcol'=32] {'fcol'}, use_global_device_ids=true, to_apply=%add.4 | all-reduce | flops 128 | bytes 1024
  449.7 1.1 rsqrt_multiply_fusion.3
  450.9 1.1 rsqrt_multiply_fusion.1
  (219 shorter events, 50.6 us)
Async XLA Ops:
  0.9 30.7 %collective-permute-start.1 = (f32[2,128,128]{2,1,0:T(8,128)S(1)}, f32[2,128,128]{2,1,0:T(8,128)S(1)}, u32[]{:S(2)}, u32[]{:S(2)}) collective-permute-start(f32[2,128,128]{2,1,0:T(8,128)S(1)} %pad_maximum_fusion.3), channel_id=1, source_target_pairs={{32,0},{64,32},{96,64},{128,96},{160,128},{192,160},{224,192},{33,... | collective-permute-start | bytes 393224 | tf_op jit(solution)/shard_map/ppermute | solution.py:24
  4.5 27.2 %collective-permute-start = (f32[2,128,128]{2,1,0:T(8,128)S(1)}, f32[2,128,128]{2,1,0:T(8,128)S(1)}, u32[]{:S(2)}, u32[]{:S(2)}) collective-permute-start(f32[2,128,128]{2,1,0:T(8,128)S(1)} %pad_maximum_fusion.3), channel_id=1, source_target_pairs={{0,32},{32,64},{64,96},{96,128},{128,160},{160,192},{192,224},{1,3... | collective-permute-start | bytes 393224 | tf_op jit(solution)/shard_map/ppermute | solution.py:21
  14.7 147.4 %copy-start.29 = (f32[1,16]{1,0:T(1,128)}, f32[1,16]{1,0:T(1,128)S(1)}, u32[]{:S(2)}) copy-start(f32[1,16]{1,0:T(1,128)S(1)} %get-tuple-element.86) | copy-start | bytes 196
  14.7 147.4 %copy-start.31 = (f32[1,16]{1,0:T(1,128)}, f32[1,16]{1,0:T(1,128)S(1)}, u32[]{:S(2)}) copy-start(f32[1,16]{1,0:T(1,128)S(1)} %get-tuple-element.87) | copy-start | bytes 196
  16.5 147.6 %copy-start.23 = (pred[158,128]{1,0:T(8,128)(4,1)}, pred[158,128]{1,0:T(8,128)(4,1)S(1)}, u32[]{:S(2)}) copy-start(pred[158,128]{1,0:T(8,128)(4,1)S(1)} %fusion.90) | copy-start | bytes 60676
  29.6 132.5 %copy-start.33 = (f32[3]{0:T(128)}, f32[3]{0:T(128)S(1)}, u32[]{:S(2)}) copy-start(f32[3]{0:T(128)S(1)} %pad.36.clone) | copy-start | bytes 40
  31.6 130.4 %copy-start.35 = (f32[16]{0:T(128)}, f32[16]{0:T(128)S(1)}, u32[]{:S(2)}) copy-start(f32[16]{0:T(128)S(1)} %get-tuple-element.92) | copy-start | bytes 196
  31.6 130.5 %copy-start.36 = (f32[16]{0:T(128)}, f32[16]{0:T(128)S(1)}, u32[]{:S(2)}) copy-start(f32[16]{0:T(128)S(1)} %get-tuple-element.93) | copy-start | bytes 196
  32.5 130.2 %collective-permute-start.3 = (f32[2,384,128]{2,1,0:T(8,128)S(1)}, f32[2,384,128]{2,1,0:T(8,128)S(1)}, u32[]{:S(2)}, u32[]{:S(2)}) collective-permute-start(f32[2,384,128]{2,1,0:T(8,128)S(1)} %pad_maximum_fusion.1), channel_id=1, source_target_pairs={{1,0},{2,1},{3,2},{4,3},{5,4},{6,5},{7,6},{8,7},{9,8},{10,9},{11,1... | collective-permute-start | bytes 1179656 | tf_op jit(solution)/shard_map/ppermute | solution.py:24
  33.8 128.9 %collective-permute-start.2 = (f32[2,384,128]{2,1,0:T(8,128)S(1)}, f32[2,384,128]{2,1,0:T(8,128)S(1)}, u32[]{:S(2)}, u32[]{:S(2)}) collective-permute-start(f32[2,384,128]{2,1,0:T(8,128)S(1)} %pad_maximum_fusion.1), channel_id=1, source_target_pairs={{0,1},{1,2},{2,3},{3,4},{4,5},{5,6},{6,7},{7,8},{8,9},{9,10},{10,1... | collective-permute-start | bytes 1179656 | tf_op jit(solution)/shard_map/ppermute | solution.py:21
  156.2 4.2 copy-start.40
  156.2 6.5 %copy-start.5 = (f32[128,128]{1,0:T(8,128)S(1)}, f32[128,128]{1,0:T(8,128)}, u32[]{:S(2)}) copy-start(f32[128,128]{1,0:T(8,128)} %param.11) | copy-start | bytes 196612
  156.3 6.5 %copy-start.6 = (f32[128,128]{1,0:T(8,128)S(1)}, f32[128,128]{1,0:T(8,128)}, u32[]{:S(2)}) copy-start(f32[128,128]{1,0:T(8,128)} %param.10) | copy-start | bytes 196612
  160.5 3.7 copy-start.7
  162.0 0.9 copy-start.38
  162.0 0.9 copy-start.39
  164.5 2.9 copy-start.21
  167.4 2.4 copy-start.2
  167.4 2.5 copy-start.4
  174.0 3.2 copy-start.24
  177.2 3.3 copy-start.22
  183.0 1.0 copy-start.1
  198.4 1.0 copy-start
  200.5 6.3 %copy-start.8 = (s32[4,128,128]{2,1,0:T(8,128)S(1)}, s32[4,128,128]{2,1,0:T(8,128)}, u32[]{:S(2)}) copy-start(s32[4,128,128]{2,1,0:T(8,128)} %param.9) | copy-start | bytes 786436
  232.0 1.8 copy-start.15
  232.0 2.3 copy-start.12
  233.8 0.9 copy-start.19
  233.8 0.9 copy-start.28
  233.8 1.5 copy-start.30
  233.8 1.5 copy-start.32
  233.8 1.5 copy-start.34
  233.9 1.5 copy-start.37
  248.3 2.2 copy-start.11
  250.0 1.4 copy-start.27
  266.2 1.8 copy-start.14
  266.2 2.2 copy-start.10
  268.0 1.4 copy-start.26
  283.9 1.8 copy-start.13
  283.9 2.2 copy-start.9
  285.7 1.4 copy-start.25
  368.9 1.0 copy-start.3
  368.9 1.0 copy-start.18
  369.0 0.9 copy-start.20
  369.0 1.6 copy-start.16
  369.0 1.6 copy-start.17
